TPU v7x, 256 devices: a whole 4x4x8 slice. The times are simulated.
256 devices in a mesh: user: 16 (over z, core), item: 16 (over y, x).
Axes of the slice: x: 4, y: 4, z: 8, core: 2. Of those that a mesh axis runs over, the one named last changes fastest.
Arguments:
- confidence: bfloat16 [384, 16, 256, 256], P('user', 'item'), may hold values from 0 to 2
- tile_rows: int32 [384, 16], P('user', 'item'), may hold values from 0 to 3
- tile_cols: int32 [384, 16], P('user', 'item'), may hold values from 0 to 7, as said below
- tile_count: int32 [16, 16], P('user', 'item'), may hold values from 1 to 24, as said below
- item_factors: bfloat16 [16, 2048, 256], P('item', 'user'), may hold values from -2 to 2
Outputs:
- user_factors: float32 [16, 1024, 256], P('user', 'item')
Inputs may be any that keep to these rules, and one draw needn't show every extreme that they name: `tile_cols`: item tile of a slot; the pairs (tile_rows, tile_cols) of one device's slots are distinct. `tile_count`: some device uses all 24 slots.
All inputs are finite; a program needn't handle non-finite values.
Results may differ from a plain program's by a relative error of at most 0.0045.
Values may be sent and summed in bfloat16 or wider, within the bound.
A program may use at most 64 MiB of HBM per device.

v0:
```python
import jax
import jax.numpy as jnp
from jax import lax
from jax.sharding import PartitionSpec as P

K = 256
TILE = 256
UTILES = 4
ITILES = 8
ITERS = 3


reg_weight = 0.1
tiny_eps = 1e-06


def shards(confidence, tile_rows, tile_cols, tile_count, item_factors):
    conf_dev = confidence[:, 0]
    rows_dev = tile_rows[:, 0]
    cols_dev = tile_cols[:, 0]
    count_dev = tile_count[0, 0]
    own_items = item_factors[0]
    group_items = lax.all_gather(item_factors, "user", axis=1, tiled=True)[0]
    gram_matrix = lax.psum(
        jnp.dot(own_items.T, own_items, preferred_element_type=jnp.float32), ("user", "item")
    )
    slots = conf_dev.shape[0]
    live_mask = jnp.arange(slots) < count_dev
    live_float = live_mask.astype(jnp.float32)
    weight_live = conf_dev * live_mask.astype(jnp.bfloat16)[:, None, None]
    y_blocks = group_items.reshape(ITILES, TILE, K)[cols_dev]
    one_hot = (rows_dev[:, None] == jnp.arange(UTILES)[None, :]).astype(jnp.float32)

    def spread_rows(contrib):
        placed = jnp.einsum("tu,tak->uak", one_hot, contrib, precision=lax.Precision.HIGHEST)
        return placed.reshape(UTILES * TILE, K)

    rhs_contrib = jnp.einsum(
        "tab,tbk->tak", weight_live, y_blocks, preferred_element_type=jnp.float32
    )
    rhs_contrib = (
        rhs_contrib
        + live_float[:, None, None] * jnp.sum(y_blocks, axis=1, dtype=jnp.float32)[:, None, :]
    )
    rhs_partial = spread_rows(rhs_contrib)

    def reduce_owned(term):
        return lax.psum_scatter(term, "item", scatter_dimension=0, tiled=True)

    rhs_vec = reduce_owned(rhs_partial)
    solution = jnp.zeros_like(rhs_vec)
    residual = rhs_vec
    direction = rhs_vec
    norm_now = jnp.sum(residual * residual, axis=-1, keepdims=True)
    for iteration in range(ITERS):
        gathered = lax.all_gather(direction.astype(jnp.bfloat16), "item", axis=0, tiled=True)
        dir_blocks = gathered.reshape(UTILES, TILE, K)[rows_dev]
        scores = jnp.einsum(
            "tak,tbk->tab", dir_blocks, y_blocks, preferred_element_type=jnp.float32
        )
        weighted = (scores * weight_live.astype(jnp.float32)).astype(jnp.bfloat16)
        tile_contrib = jnp.einsum(
            "tab,tbk->tak", weighted, y_blocks, preferred_element_type=jnp.float32
        )
        image = (
            reduce_owned(spread_rows(tile_contrib))
            + jnp.dot(direction, gram_matrix, precision=lax.Precision.HIGHEST)
            + reg_weight * direction
        )
        alpha = norm_now / (jnp.sum(direction * image, axis=-1, keepdims=True) + tiny_eps)
        solution = solution + alpha * direction
        residual = residual - alpha * image
        if iteration + 1 < ITERS:
            norm_next = jnp.sum(residual * residual, axis=-1, keepdims=True)
            direction = residual + norm_next / (norm_now + tiny_eps) * direction
            norm_now = norm_next
    return solution[None]


def solution(mesh):
    in_specs = (
        P("user", "item", None, None),
        P("user", "item"),
        P("user", "item"),
        P("user", "item"),
        P("item", "user", None),
    )
    out_specs = P("user", "item", None)
    return jax.shard_map(shards, mesh=mesh, in_specs=in_specs, out_specs=out_specs, check_vma=False)
```

profile of v0, /device:TPU:2, one launch (start us, length us, event | category | flops | bytes accessed | tf_op | source)
XLA Modules:
  0.0 585.4 jit_solution(17161731033642096363)
XLA Ops:
  7.4 0.7 all-gather.2.cloned.1.call-update
  8.1 0.0 reduce-scatter.5.cloned.1.call-start
  8.8 0.7 fusion.36
  9.5 42.1 %all-gather.2.cloned.1.call-done = bf16[1,2048,256]{2,1,0:T(8,128)(2,1)} async-done(((bf16[1,128,256]{2,1,0:T(8,128)(2,1)}), bf16[1,2048,256]{2,1,0:T(8,128)(2,1)}) %all-gather.2.cloned.1.call-update) | async-done | bytes 1048592 | tf_op jit(solution)/shard_map/all_gather | solution.py:23
  51.5 2.0 gather_fusion
  53.5 0.0 copy-start
  53.5 0.4 convert_reduce_fusion
  54.0 0.1 broadcast_multiply_fusion
  54.1 1.4 copy-done
  55.4 1.0 fusion.23
  56.5 5.7 fusion.9
  62.1 0.0 copy-start.5
  62.2 1.2 copy.8
  63.3 0.0 reduce-scatter.5.cloned.1.call-update
  63.4 0.0 all-reduce.2.cloned.1.call-start
  63.4 0.9 fusion.33
  64.3 0.0 all-reduce.2.cloned.1.call-update
  64.4 0.0 reduce-scatter.7.cloned.1.call-start
  64.4 76.2 %reduce-scatter.5.cloned.1.call-done = f32[64,256]{1,0:T(8,128)} async-done(((f32[1024,256]{1,0:T(8,128)}), f32[64,256]{1,0:T(8,128)}) %reduce-scatter.5.cloned.1.call-update) | async-done | bytes 65552 | tf_op jit(solution)/shard_map/reduce_scatter | solution.py:48
  140.7 0.8 convert_element_type.44
  141.5 24.4 %all_gather.13 = bf16[1024,256]{1,0:T(8,128)(2,1)} all-gather(bf16[64,256]{1,0:T(8,128)(2,1)S(1)} %convert_element_type.44), channel_id=1, replica_groups=mesh['user'=16,'item'=16] {'item'}, dimensions={0}, use_global_device_ids=true | all-gather | bytes 557056 | tf_op jit(solution)/shard_map/all_gather | solution.py:56
  165.9 3.6 gather_fusion.1
  169.5 7.4 %fusion.14 = f32[24,256,256]{2,1,0:T(8,128)} fusion(bf16[24,256,256]{2,1,0:T(8,128)(2,1)S(1)} %gather_fusion, bf16[24,256,256]{2,1,0:T(8,128)(2,1)} %gather_fusion.1, bf16[24,1,256,256]{3,2,1,0:T(8,128)(2,1)} %param.5, bf16[24]{0:T(256)(128)(2,1)S(1)} %get-tuple-element.17), kind=kOutput, calls=%fused_computation.21 | convolution fusion | flops 1616904192 | bytes 15728688 | tf_op jit(solution)/shard_map/tab,tbk->tak/dot_general | solution.py:62
  177.0 8.3 %fusion.7 = f32[4,256,256]{2,0,1:T(4,128)S(1)} fusion(f32[24,256,256]{2,1,0:T(8,128)} %fusion.14, s32[24]{0:T(128)S(1)} %bitcast.63), kind=kOutput, calls=%fused_computation.14 | convolution fusion | flops 75497568 | bytes 7340128 | tf_op jit(solution)/shard_map/tu,tak->uak/dot_general | solution.py:35
  185.3 1.2 copy.9
  186.5 0.0 reduce-scatter.7.cloned.1.call-update
  186.5 0.0 reduce-scatter.9.cloned.1.call-start
  186.5 135.9 %all-reduce.2.cloned.1.call-done = f32[256,256]{1,0:T(8,128)} async-done(((f32[256,256]{1,0:T(8,128)}), f32[256,256]{1,0:T(8,128)}) %all-reduce.2.cloned.1.call-update) | async-done | bytes 262160 | tf_op jit(solution)/shard_map/psum | solution.py:24
  322.5 0.0 copy-done.2
  322.5 1.3 multiply_reduce_fusion.3
  323.8 0.0 copy-start.7
  323.8 0.2 multiply_reduce_fusion.2
  324.0 0.0 copy-start.9
  324.0 0.4 copy-done.7
  324.4 0.1 copy-done.9
  324.5 0.7 fusion.43
  325.2 25.5 %all_gather.14 = bf16[1024,256]{1,0:T(8,128)(2,1)} all-gather(bf16[64,256]{1,0:T(8,128)(2,1)S(1)} %get-tuple-element.9), channel_id=1, replica_groups=mesh['user'=16,'item'=16] {'item'}, dimensions={0}, use_global_device_ids=true | all-gather | bytes 557056 | tf_op jit(solution)/shard_map/all_gather | solution.py:56
  350.7 3.6 gather_fusion.2
  354.3 7.4 %fusion.12 = f32[24,256,256]{2,1,0:T(8,128)} fusion(bf16[24,256,256]{2,1,0:T(8,128)(2,1)S(1)} %gather_fusion, bf16[24,256,256]{2,1,0:T(8,128)(2,1)} %gather_fusion.2, bf16[24,1,256,256]{3,2,1,0:T(8,128)(2,1)} %param.5, bf16[24]{0:T(256)(128)(2,1)S(1)} %get-tuple-element.17), kind=kOutput, calls=%fused_computation.20 | convolution fusion | flops 1616904192 | bytes 15728688 | tf_op jit(solution)/shard_map/tab,tbk->tak/dot_general | solution.py:62
  361.7 8.3 %fusion.5 = f32[4,256,256]{2,0,1:T(4,128)S(1)} fusion(f32[24,256,256]{2,1,0:T(8,128)} %fusion.12, s32[24]{0:T(128)S(1)} %bitcast.64), kind=kOutput, calls=%fused_computation.12 | convolution fusion | flops 75497568 | bytes 7340128 | tf_op jit(solution)/shard_map/tu,tak->uak/dot_general | solution.py:35
  370.0 1.2 copy.10
  371.2 0.0 reduce-scatter.9.cloned.1.call-update
  371.2 0.0 reduce-scatter.11.cloned.1.call-start
  371.3 76.3 %reduce-scatter.9.cloned.1.call-done = f32[64,256]{1,0:T(8,128)} async-done(((f32[1024,256]{1,0:T(8,128)}), f32[64,256]{1,0:T(8,128)}) %reduce-scatter.9.cloned.1.call-update) | async-done | bytes 65552 | tf_op jit(solution)/shard_map/reduce_scatter | solution.py:48
  447.6 1.3 multiply_reduce_fusion.1
  448.9 0.6 add_divide_fusion.2
  449.5 0.2 multiply_reduce_fusion
  449.7 0.0 copy-start.10
  449.7 0.5 copy-done.10
  450.2 0.6 add_divide_fusion.1
  450.8 1.6 fusion.42
  452.3 24.5 %all_gather.15 = bf16[1024,256]{1,0:T(8,128)(2,1)} all-gather(bf16[64,256]{1,0:T(8,128)(2,1)S(1)} %get-tuple-element.7), channel_id=1, replica_groups=mesh['user'=16,'item'=16] {'item'}, dimensions={0}, use_global_device_ids=true | all-gather | bytes 557056 | tf_op jit(solution)/shard_map/all_gather | solution.py:56
  476.8 3.6 gather_fusion.3
  480.4 7.4 %fusion.10 = f32[24,256,256]{2,1,0:T(8,128)} fusion(bf16[24,256,256]{2,1,0:T(8,128)(2,1)S(1)} %gather_fusion, bf16[24,256,256]{2,1,0:T(8,128)(2,1)} %gather_fusion.3, bf16[24,1,256,256]{3,2,1,0:T(8,128)(2,1)} %param.5, bf16[24]{0:T(256)(128)(2,1)S(1)} %get-tuple-element.17), kind=kOutput, calls=%fused_computation.19 | convolution fusion | flops 1616904192 | bytes 15728688 | tf_op jit(solution)/shard_map/tab,tbk->tak/dot_general | solution.py:62
  487.8 8.3 %fusion.3 = f32[4,256,256]{2,0,1:T(4,128)S(1)} fusion(f32[24,256,256]{2,1,0:T(8,128)} %fusion.10, s32[24]{0:T(128)S(1)} %bitcast.65), kind=kOutput, calls=%fused_computation.10 | convolution fusion | flops 75497568 | bytes 7340128 | tf_op jit(solution)/shard_map/tu,tak->uak/dot_general | solution.py:35
  496.1 0.0 copy-start.4
  496.1 0.0 copy-start.11
  496.1 0.0 copy-start.3
  496.1 1.2 copy.11
  497.3 0.0 reduce-scatter.11.cloned.1.call-update
  497.3 78.9 %reduce-scatter.11.cloned.1.call-done = f32[64,256]{1,0:T(8,128)} async-done(((f32[1024,256]{1,0:T(8,128)}), f32[64,256]{1,0:T(8,128)}) %reduce-scatter.11.cloned.1.call-update) | async-done | bytes 65552 | tf_op jit(solution)/shard_map/reduce_scatter | solution.py:48
  576.3 0.0 copy-done.4
  576.3 1.2 fusion.32
  577.5 0.7 add_bitcast_fusion
  (19 shorter events, 0.1 us)
Async XLA Ops:
  7.4 44.2 %all-gather.2.cloned.1.call-start = ((), (), s32[]{:S(2)}) async-start(), calls=%async_computation.4 | async-start | bytes 1114112 | tf_op jit(solution)/shard_map/all_gather | solution.py:23
  8.1 132.6 %reduce-scatter.5.cloned.1.call-start = ((), (), s32[]{:S(2)}) async-start(), calls=%async_computation.5 | async-start | bytes 1114112 | tf_op jit(solution)/shard_map/reduce_scatter | solution.py:48
  53.5 1.9 copy-start
  55.4 1.1 copy-start.6
  62.1 1.3 copy-start.5
  63.4 259.1 %all-reduce.2.cloned.1.call-start = ((), (), s32[]{:S(2)}) async-start(), calls=%async_computation.7 | async-start | bytes 524288 | tf_op jit(solution)/shard_map/psum | solution.py:24
  64.4 258.1 %reduce-scatter.7.cloned.1.call-start = ((), (), s32[]{:S(2)}) async-start(), calls=%async_computation.6 | async-start | bytes 1114112 | tf_op jit(solution)/shard_map/reduce_scatter | solution.py:48
  185.3 137.2 %copy-start.2 = (f32[64,256]{1,0:T(8,128)S(1)}, f32[64,256]{1,0:T(8,128)}, u32[]{:S(2)}) copy-start(f32[64,256]{1,0:T(8,128)} %reduce-scatter.5.cloned.1.call-done) | copy-start | bytes 196612
  186.5 261.1 %reduce-scatter.9.cloned.1.call-start = ((), (), s32[]{:S(2)}) async-start(), calls=%async_computation.8 | async-start | bytes 1114112 | tf_op jit(solution)/shard_map/reduce_scatter | solution.py:48
  323.8 0.6 copy-start.7
  324.0 0.5 copy-start.9
  370.0 77.6 %copy-start.1 = (f32[256,256]{1,0:T(8,128)S(1)}, f32[256,256]{1,0:T(8,128)}, u32[]{:S(2)}) copy-start(f32[256,256]{1,0:T(8,128)} %all-reduce.2.cloned.1.call-done) | copy-start | bytes 786436
  371.2 205.0 %reduce-scatter.11.cloned.1.call-start = ((), (), s32[]{:S(2)}) async-start(), calls=%async_computation.9 | async-start | bytes 1114112 | tf_op jit(solution)/shard_map/reduce_scatter | solution.py:48
  449.7 0.5 copy-start.10
  496.1 80.2 %copy-start.4 = (f32[64,256]{1,0:T(8,128)S(1)}, f32[64,256]{1,0:T(8,128)}, u32[]{:S(2)}) copy-start(f32[64,256]{1,0:T(8,128)} %get-tuple-element.8) | copy-start | bytes 196612
  496.1 81.3 %copy-start.11 = (f32[64]{0:T(128)S(1)}, f32[64]{0:T(128)}, u32[]{:S(2)}) copy-start(f32[64]{0:T(128)} %copy-done.10) | copy-start | bytes 772
  496.1 81.4 %copy-start.3 = (f32[64,256]{1,0:T(8,128)S(1)}, f32[64,256]{1,0:T(8,128)}, u32[]{:S(2)}) copy-start(f32[64,256]{1,0:T(8,128)} %get-tuple-element.10) | copy-start | bytes 196612
  496.1 81.4 %copy-start.8 = (f32[64]{0:T(128)S(1)}, f32[64]{0:T(128)}, u32[]{:S(2)}) copy-start(f32[64]{0:T(128)} %copy-done.7) | copy-start | bytes 772
Sparse Core Ops, SparseCore 0:
  10.0 41.4 all-gather.1
  63.5 77.1 reduce-scatter.4
  186.6 78.8 reduce-scatter.6
  371.3 76.2 reduce-scatter.8
  497.5 78.7 reduce-scatter.10
Sparse Core Ops, SparseCore 1:
  69.3 253.1 all-reduce.1
where the time goes:
time: 586 us; the launch traced here: 585 us
  waiting for transfers between devices  410 us (70%)
  blocking collectives  74.5 us (13%)
  matrix products  58.5 us (10%)
  local copies, waits for them, and re-layouts  19.8 us (3%)
  between operations  15.5 us (3%)
  other arithmetic  6.57 us (1%)
    reduce_scatter x4, waiting for transfers between devices, reduce_owned(): return lax.psum_scatter(term, 'item', scatter_dimension=0, tiled=True)  231 us
    psum x1, waiting for transfers between devices, shards(): lax.psum(jnp.dot(own_items.T, own_items, preferred_element_type=jnp.float...  136 us
    all_gather x3, blocking collectives, shards(): lax.all_gather(direction.astype(jnp.bfloat16), 'item', axis=0, tiled=True)  74.5 us
    all_gather x1, waiting for transfers between devices, shards(): group_items = lax.all_gather(item_factors, 'user', axis=1, tiled=True)[0]  42.1 us
    dot_general x4, matrix products, spread_rows(): jnp.einsum('tu,tak->uak', one_hot, contrib, precision=lax.Precision.HIGHEST)  30.5 us
    dot_general x3, matrix products, shards(): jnp.einsum('tab,tbk->tak', weighted, y_blocks, preferred_element_type=jnp...  22.3 us
  transfers between devices with their start and end apart: 6, of which 5 were waited for; matrix products, arithmetic and copies ran while one was open for 4% of the time, Pallas kernels for 0%

commit v1 on v0

v1 whole, which is shorter than its diff:
```python
import jax
import jax.numpy as jnp
from jax import lax
from jax.experimental import pallas as pl
from jax.experimental.pallas import tpu as pltpu
from jax.sharding import PartitionSpec as P

K = 256
TILE = 256
UTILES = 4
ITILES = 8
MAXT = 24
OWN = 64
SIDE = 4
PLANE = SIDE * SIDE
RING = 8
SHARD = 128
USERS = UTILES * TILE
ITEMS = ITILES * TILE
ROWS = K // PLANE

reg_weight = 0.1
tiny_eps = 1e-6

MESH = pl.DeviceIdType.MESH
F32 = jnp.float32
BF16 = jnp.bfloat16
HIGH = lax.Precision.HIGHEST


def blk(index, size):
    return pl.ds(pl.multiple_of(index * size, size), size)


def kernel(rows_ref, cols_ref, count_ref, conf_hbm, items_ref, out_ref,
           conf, yall, w, tbuf, dall, part, rbuf, qloc, qbuf,
           gfull, gpart, gown, gram, msum, colsum,
           sol, res, dirv, rr,
           keys, slots, lives,
           conf_sem, up_s, up_r, dn_s, dn_r, pa_s, pa_r,
           ag_s, ag_r, rs_s, rs_r, q_s, q_r, gp_s, gp_r, gz_s, gz_r):
    a = lax.axis_index("user")
    b = lax.axis_index("item")
    z, core = a // 2, a % 2
    y, x = b // SIDE, b % SIDE

    conf_copy = pltpu.make_async_copy(conf_hbm, conf, conf_sem)
    conf_copy.start()

    def plane(k):
        return ((y + k // SIDE) % SIDE) * SIDE + (x + k % SIDE) % SIDE

    def plane_from(k):
        return ((y + SIDE - k // SIDE) % SIDE) * SIDE + (x + SIDE - k % SIDE) % SIDE

    def group(j):
        return (a + j) % PLANE

    def group_from(j):
        return (a + PLANE - j) % PLANE

    def each(body):
        @pl.loop(1, PLANE)
        def _(k):
            body(k)

    def remote(src, dst, ssem, rsem, where):
        return pltpu.make_async_remote_copy(
            src_ref=src, dst_ref=dst, send_sem=ssem, recv_sem=rsem,
            device_id=where, device_id_type=MESH)

    barrier = pltpu.get_barrier_semaphore()

    def greet(k):
        pl.semaphore_signal(barrier, inc=1, device_id={"item": plane(k)}, device_id_type=MESH)
        pl.semaphore_signal(barrier, inc=1, device_id={"user": group(k)}, device_id_type=MESH)

    each(greet)

    for s in range(MAXT):
        live = s < count_ref[0, 0]
        keys[s] = jnp.where(live, rows_ref[s, 0] * ITILES + cols_ref[s, 0], -1)

    @pl.loop(0, UTILES * ITILES)
    def _(p):
        slot = jnp.int32(0)
        live = jnp.int32(0)
        for s in range(MAXT):
            hit = (keys[s] == p).astype(jnp.int32)
            slot = slot + s * hit
            live = live + hit
        slots[p] = slot
        lives[p] = live

    pl.semaphore_wait(barrier, 2 * (PLANE - 1))

    def shard(r, c):
        return ((z + r) % RING) * 2 + c

    def rows_of(r, c, first, size):
        return yall.at[pl.ds(pl.multiple_of(shard(r, c) * SHARD + first, 64), size)]

    def span(h, upward):
        if h < RING // 2:
            return 0, SHARD
        return (0, SHARD // 2) if upward else (SHARD // 2, SHARD // 2)

    def hop(h, upward, arriving):
        first, size = span(h, upward)
        r = (-1 if upward else 1) * (h if arriving else h - 1)
        r = (r + RING) % RING
        there = rows_of(r, core, first, size)
        src = there
        if h == 1 and not arriving:
            src = items_ref
        target = (z + (1 if upward else RING - 1)) % RING
        sems = (up_s, up_r) if upward else (dn_s, dn_r)
        return remote(src, there, sems[0].at[h], sems[1].at[h], {"user": target * 2 + core})

    def to_partner(r, arriving=False):
        there = rows_of(r, 1 - core if arriving else core, 0, SHARD)
        src = items_ref if (r == 0 and not arriving) else there
        return remote(src, there, pa_s.at[r], pa_r.at[r], {"user": z * 2 + 1 - core})

    hop(1, True, False).start()
    hop(1, False, False).start()
    to_partner(0).start()
    yall[blk(shard(0, core), SHARD), :] = items_ref[...]
    conf_copy.wait()

    def spread(u):
        @pl.loop(0, ITILES)
        def _(c):
            p = u * ITILES + c
            scale = lives[p].astype(F32).astype(BF16)
            w[u, :, blk(c, TILE)] = conf[slots[p]] * scale

    for h in range(1, RING // 2 + 1):
        spread(h - 1)
        hop(h, True, True).wait_recv()
        if h < RING // 2:
            hop(h + 1, True, False).start()
            to_partner(RING - h).start()
        hop(h, False, True).wait_recv()
        if h < RING // 2:
            hop(h + 1, False, False).start()
            to_partner(h).start()
        else:
            to_partner(RING // 2).start()
    for r in range(RING):
        to_partner(r, True).wait_recv()
    for h in range(1, RING // 2 + 1):
        hop(h, True, False).wait_send()
        hop(h, False, False).wait_send()
    for r in range(RING):
        to_partner(r).wait_send()

    for c in range(ITILES):
        colsum[c] = jnp.dot(jnp.ones((8, TILE), BF16), yall[c * TILE:(c + 1) * TILE, :],
                            preferred_element_type=F32)

    def own_rows(ref, who):
        return ref.at[blk(who, OWN)]

    def rs_send(k):
        return remote(own_rows(part, plane(k)), rbuf.at[k], rs_s.at[k], rs_r.at[k], {"item": plane(k)})

    def q_send(k):
        return remote(qloc.at[plane(k) // SIDE], qbuf.at[k], q_s.at[k], q_r.at[k], {"item": plane(k)})

    def ag_send(k):
        return remote(own_rows(dall, b), own_rows(dall, b), ag_s.at[k], ag_r.at[k], {"item": plane(k)})

    def ag_recv(k):
        who = plane_from(k)
        return remote(own_rows(dall, who), own_rows(dall, who), ag_s.at[k], ag_r.at[k], {"item": who})

    def gp_send(k):
        return remote(gfull.at[blk(a, ROWS)], gpart.at[k], gp_s.at[k], gp_r.at[k], {"item": plane(k)})

    def gz_send(j):
        return remote(gown, gram.at[blk(a, ROWS)], gz_s.at[j], gz_r.at[j], {"user": group(j)})

    def gz_recv(j):
        who = group_from(j)
        return remote(gown, gram.at[blk(who, ROWS)], gz_s.at[j], gz_r.at[j], {"user": who})

    def step_of(t):
        return (t * (t + 1) // 2) % SIDE

    def to_owners(t, send):
        for i in range(SIDE):
            k = step_of(t) * SIDE + i

            @pl.when(k != 0)
            def _():
                send(k).start()

    @pl.loop(0, UTILES)
    def _(t):
        u = (y + step_of(t)) % SIDE
        total = jnp.dot(w[u], yall[...], preferred_element_type=F32)
        base = jnp.zeros((8, K), F32)
        for c in range(ITILES):
            base = base + lives[u * ITILES + c].astype(F32) * colsum[c]
        msum[...] = base
        part[blk(u, TILE), :] = total + msum[0:1, :]
        to_owners(t, rs_send)

    gfull[...] = lax.dot_general(yall[...], yall[...], (((0,), (0,)), ((), ())), preferred_element_type=F32)
    each(lambda k: gp_send(k).start())

    def collect():
        res_own = part[blk(b, OWN), :]

        def add(k, total):
            rs_send(k).wait_recv()
            return total + rbuf[k]

        total = lax.fori_loop(1, PLANE, add, res_own)
        each(lambda k: rs_send(k).wait_send())
        return total

    def row_sum(v):
        return jnp.sum(v, axis=-1, keepdims=True)

    rhs = collect()
    sol[...] = jnp.zeros_like(sol)
    res[...] = rhs
    dirv[...] = rhs
    rr[...] = jnp.broadcast_to(row_sum(rhs * rhs), rr.shape)

    def share():
        dall[blk(b, OWN), :] = dirv[...].astype(BF16)
        each(lambda k: ag_send(k).start())

    def await_row(t):
        back = (SIDE - step_of(t)) % SIDE
        for i in range(SIDE):
            k = back * SIDE + i

            @pl.when(k != 0)
            def _():
                ag_recv(k).wait_recv()

    share()

    def add_gram(k, total):
        gp_send(k).wait_recv()
        return total + gpart[k]

    gown[...] = lax.fori_loop(1, PLANE, add_gram, gfull[blk(a, ROWS), :])
    each(lambda k: gz_send(k).start())
    gram[blk(a, ROWS), :] = gown[...]
    each(lambda k: gp_send(k).wait_send())

    def scores(u, c):
        return lax.dot_general(dall[blk(u, TILE), :], yall[c * TILE:(c + 1) * TILE, :],
                               (((1,), (1,)), ((), ())), preferred_element_type=F32)

    @pl.loop(0, 2)
    def _(it):
        @pl.loop(0, UTILES)
        def _(t):
            u = (y + step_of(t)) % SIDE
            await_row(t)
            for c in range(ITILES):
                cols = slice(c * TILE, (c + 1) * TILE)
                tbuf[:, cols] = (scores(u, c) * w[u, :, cols].astype(F32)).astype(BF16)
            part[blk(u, TILE), :] = jnp.dot(tbuf[...], yall[...], preferred_element_type=F32)
            to_owners(t, rs_send)

        @pl.when(it == 0)
        def _():
            each(lambda k: gz_recv(k).wait_recv())
            each(lambda k: gz_send(k).wait_send())

        d = dirv[...]
        dense = jnp.dot(d, gram[...], precision=HIGH, preferred_element_type=F32) + reg_weight * d
        each(lambda k: ag_send(k).wait_send())
        image = collect() + dense
        norm = rr[:, 0:1]
        alpha = norm / (row_sum(d * image) + tiny_eps)
        sol[...] = sol[...] + alpha * d
        left = res[...] - alpha * image
        res[...] = left
        new = row_sum(left * left)
        dirv[...] = left + new / (norm + tiny_eps) * d
        rr[...] = jnp.broadcast_to(new, rr.shape)
        share()

    ones = jnp.ones((8, 128), F32)

    @pl.loop(0, UTILES)
    def _(t):
        u = (y + step_of(t)) % SIDE
        await_row(t)
        lanes = jnp.zeros((TILE, 128), F32)
        for c in range(ITILES):
            cols = slice(c * TILE, (c + 1) * TILE)
            s = scores(u, c)
            prod = (s * w[u, :, cols].astype(F32)).astype(BF16).astype(F32) * s
            lanes = lanes + prod[:, :128] + prod[:, 128:]
        qloc[u] = lax.dot_general(ones, lanes, (((1,), (1,)), ((), ())), precision=HIGH,
                                  preferred_element_type=F32)
        to_owners(t, q_send)

    d = dirv[...]
    dense = jnp.dot(d, gram[...], precision=HIGH, preferred_element_type=F32) + reg_weight * d
    own = row_sum(d * dense)
    each(lambda k: ag_send(k).wait_send())

    def add_q(k, total):
        q_send(k).wait_recv()
        return total + qbuf[k]

    q = lax.fori_loop(1, PLANE, add_q, qloc[y])
    each(lambda k: q_send(k).wait_send())
    msum[...] = q
    wide = jnp.broadcast_to(msum[0:1, :], (OWN, TILE))
    lane = lax.broadcasted_iota(jnp.int32, (OWN, TILE), 1)
    row = lax.broadcasted_iota(jnp.int32, (OWN, TILE), 0)
    tiles = row_sum(jnp.where(lane == row + x * OWN, wide, 0.0))
    alpha = rr[:, 0:1] / (tiles + own + tiny_eps)
    out_ref[...] = sol[...] + alpha * d


def shards(confidence, tile_rows, tile_cols, tile_count, item_factors):
    vmem = pl.BlockSpec(memory_space=pltpu.VMEM)
    smem = pl.BlockSpec(memory_space=pltpu.SMEM)
    dma = pltpu.SemaphoreType.DMA
    out = pl.pallas_call(
        kernel,
        out_shape=jax.ShapeDtypeStruct((OWN, K), F32),
        in_specs=[smem, smem, smem, pl.BlockSpec(memory_space=pl.ANY), vmem],
        out_specs=vmem,
        scratch_shapes=[
            pltpu.VMEM((MAXT, TILE, TILE), BF16),
            pltpu.VMEM((ITEMS, K), BF16),
            pltpu.VMEM((UTILES, TILE, ITEMS), BF16),
            pltpu.VMEM((TILE, ITEMS), BF16),
            pltpu.VMEM((USERS, K), BF16),
            pltpu.VMEM((USERS, K), F32),
            pltpu.VMEM((PLANE, OWN, K), F32),
            pltpu.VMEM((UTILES, 8, TILE), F32),
            pltpu.VMEM((PLANE, 8, TILE), F32),
            pltpu.VMEM((K, K), F32),
            pltpu.VMEM((PLANE, ROWS, K), F32),
            pltpu.VMEM((ROWS, K), F32),
            pltpu.VMEM((K, K), F32),
            pltpu.VMEM((8, K), F32),
            pltpu.VMEM((ITILES, 8, K), F32),
            pltpu.VMEM((OWN, K), F32),
            pltpu.VMEM((OWN, K), F32),
            pltpu.VMEM((OWN, K), F32),
            pltpu.VMEM((OWN, 128), F32),
            pltpu.SMEM((MAXT,), jnp.int32),
            pltpu.SMEM((UTILES * ITILES,), jnp.int32),
            pltpu.SMEM((UTILES * ITILES,), jnp.int32),
            dma,
            dma((5,)), dma((5,)), dma((5,)), dma((5,)), dma((RING,)), dma((RING,)),
        ] + [dma((PLANE,))] * 10,
        compiler_params=pltpu.CompilerParams(
            collective_id=0, has_side_effects=True, vmem_limit_bytes=60 * 1024 * 1024),
    )(tile_rows, tile_cols, tile_count, confidence.reshape(MAXT, TILE, TILE), item_factors[0])
    return out[None]


def solution(mesh):
    in_specs = (
        P("user", "item", None, None),
        P("user", "item"),
        P("user", "item"),
        P("user", "item"),
        P("item", "user", None),
    )
    out_specs = P("user", "item", None)
    return jax.shard_map(shards, mesh=mesh, in_specs=in_specs, out_specs=out_specs, check_vma=False)
```

time: 586 us -> 114 us (0.19)
  waiting for transfers between devices: 410 us -> 0 us
  Pallas kernels: 0 us -> 107 us
  blocking collectives: 74.5 us -> 0 us
  matrix products: 58.5 us -> 0 us
  local copies, waits for them, and re-layouts: 19.8 us -> 4.14 us
  between operations: 15.5 us -> 0.66 us
  other arithmetic: 6.57 us -> 0 us
    reduce_scatter x4 -> x0, waiting for transfers between devices: 231 us -> none  [reduce_owned(): return lax.psum_scatter(term, 'item', scatter_dimension=0, tiled=True)]
    psum x1 -> x0, waiting for transfers between devices: 136 us -> none  [shards(): lax.psum(jnp.dot(own_items.T, own_items, preferred_element_type=jnp.float...]
    pallas_call x0 -> x1, Pallas kernels: none -> 107 us  [shards(): pl.pallas_call(kernel, out_shape=jax.ShapeDtypeStruct((OWN, K), F32), in_...]
    all_gather x3 -> x0, blocking collectives: 74.5 us -> none  [shards(): lax.all_gather(direction.astype(jnp.bfloat16), 'item', axis=0, tiled=True)]
    dot_general x12 -> x0, matrix products: 58.5 us -> none  [the longest x4 30.5 us: spread_rows(): jnp.einsum('tu,tak->uak', one_hot, contrib, precision=lax.Precision.HIGHEST)]
    all_gather x1 -> x0, waiting for transfers between devices: 42.1 us -> none  [shards(): group_items = lax.all_gather(item_factors, 'user', axis=1, tiled=True)[0]]
    gather x4 -> x0, local copies, waits for them, and re-layouts: 12.7 us -> none  [the longest x3 10.8 us: shards(): dir_blocks = gathered.reshape(UTILES, TILE, K)[rows_dev]]
  transfers between devices with their start and end apart: 6 -> 0, of which waited for: 5 -> 0; matrix products, arithmetic and copies ran while one was open for 4% -> 0% of each run, Pallas kernels for 0% -> 0%
where the time goes in v1:
time: 114 us; the launch traced here: 112 us
  Pallas kernels  107 us (94%)
  local copies, waits for them, and re-layouts  4.14 us (4%)
    pallas_call x1, Pallas kernels, shards(): pl.pallas_call(kernel, out_shape=jax.ShapeDtypeStruct((OWN, K), F32), in_...  107 us
    unnamed x3, local copies, waits for them, and re-layouts  4.14 us

profile of v1, /device:TPU:2, one launch (start us, length us, event | category | flops | bytes accessed | tf_op | source)
XLA Modules:
  0.0 111.9 jit_solution(11988038636061541298)
XLA Ops:
  0.7 1.3 %copy.6.rows_ref = s32[24,1]{1,0:T(8,128)} copy(s32[24,1]{0,1:T(1,128)} %param.6) | data formatting | bytes 192 | tf_op args[1]
  2.0 1.3 %copy.7.cols_ref = s32[24,1]{1,0:T(8,128)} copy(s32[24,1]{0,1:T(1,128)} %param.7) | data formatting | bytes 192 | tf_op args[2]
  3.3 107.1 %shard_map.55 = f32[64,256]{1,0:T(8,128)} custom-call(s32[24,1]{1,0:T(8,128)} %copy.6.rows_ref, s32[24,1]{1,0:T(8,128)} %copy.7.cols_ref, s32[1,1]{1,0:T(1,128)S(6)} %copy.9.count_ref, bf16[24,256,256]{2,1,0:T(8,128)(2,1)} %bitcast.3, bf16[128,256]{1,0:T(8,128)(2,1)} %bitcast.5), custom_call_target="tpu_custom_call" | custom-call | tf_op jit(solution)/shard_map/pallas_call | solution.py:332
  110.4 1.5 %copy.10 = f32[1,64,256]{2,1,0:T(8,128)} copy(f32[1,64,256]{2,1,0:T(8,128)} %bitcast.4) | data formatting | bytes 131072
